TPU v7x, 128 devices: a whole 4x4x4 slice. The times are simulated.
128 devices in a mesh: row: 16 (over x, z), col: 8 (over y, core).
Axes of the slice: x: 4, y: 4, z: 4, core: 2. Of those that a mesh axis runs over, the one named last changes fastest.
Arguments:
- qkv: bfloat16 [3, 1408, 32768], P(None, 'col', 'row'), may hold values from -12.1 to 12.1
- residual_in: bfloat16 [1408, 32768], P('col', 'row'), may hold values from -3 to 3
- out_weight: bfloat16 [1408, 1408], replicated, may hold values from -0.625 to 0.625
- merge_weight: bfloat16 [1408, 5632], P('col'), may hold values from -0.078125 to 0.078125
- merge_gain: float32 [1408], replicated, may hold values from 0.1 to 1.9
- image_groups: int32 [64], replicated, may hold values from 1 to 256, 8192 in all
- dest_row: int32 [8192], P('row'), may hold values from 0 to 8191, as said below
Outputs:
- layer_out: bfloat16 [1408, 32768], P('col', 'row')
- image_rows: bfloat16 [1408, 8192], P('col', 'row')
Inputs may be any that keep to these rules, and one draw needn't show every extreme that they name: dest_row is a permutation of 0 to 8191. Of the 512 entries held by each index of row, exactly 32 fall in each aligned block of 512 output rows.
All inputs are finite; a program needn't handle non-finite values.
Results may differ from a plain program's by a relative error of at most 0.0064.
Values may be sent and summed in bfloat16 or wider, within the bound.
A program may use at most 128 MiB of HBM per device.

v0:
```python
import math
import jax
import jax.numpy as jnp
from jax import lax
from jax.sharding import PartitionSpec as P

HEAD_DIM = 88


def with_halo(cells, sides, width):
    for axis, dim in sides:
        count = lax.axis_size(axis)
        ends = count - 1
        head = lax.slice_in_dim(cells, 0, width, axis=dim)
        tail = lax.slice_in_dim(cells, cells.shape[dim] - width, cells.shape[dim], axis=dim)
        cells = jnp.concatenate(
            [
                lax.ppermute(tail, axis, [(i, (i + 1) % count) for i in range(ends)]),
                cells,
                lax.ppermute(head, axis, [((i + 1) % count, i) for i in range(ends)]),
            ],
            axis=dim,
        )
    return cells


def image_labels(positions, image_ends, all_tokens):
    inside = (positions >= 0) & (positions < all_tokens)
    counted = jnp.sum((positions[:, None] >= image_ends[None, :]).astype(jnp.int32), axis=1)
    return jnp.where(inside, counted, -1)


def body(qkv, residual_in, out_weight, merge_weight, merge_gain, image_groups, dest_row):
    width_here = qkv.shape[1]
    tok_rows = qkv.shape[2]
    heads_here = width_here // HEAD_DIM
    full_width = out_weight.shape[0]
    reach_rows = tok_rows // 2
    block_rows = min(1024, tok_rows)
    block_count = tok_rows // block_rows
    window = block_rows + 2 * reach_rows
    row_count = lax.axis_size("row")
    row_id = lax.axis_index("row")
    col_id = lax.axis_index("col")
    all_tokens = tok_rows * row_count
    score_scale = 1.0 / math.sqrt(HEAD_DIM)
    image_ends = jnp.cumsum(image_groups) * 4
    extended = with_halo(qkv[1:], (("row", 2),), reach_rows)
    positions = (
        row_id * tok_rows - reach_rows + jnp.arange(tok_rows + 2 * reach_rows, dtype=jnp.int32)
    )
    labels = image_labels(positions, image_ends, all_tokens)

    def attend(block_id):
        first_row = block_id * block_rows
        queries = lax.dynamic_slice_in_dim(qkv[0], first_row, block_rows, 1).reshape(
            heads_here, HEAD_DIM, block_rows
        )
        key_block = lax.dynamic_slice_in_dim(extended[0], first_row, window, 1).reshape(
            heads_here, HEAD_DIM, window
        )
        value_block = lax.dynamic_slice_in_dim(extended[1], first_row, window, 1).reshape(
            heads_here, HEAD_DIM, window
        )
        query_labels = lax.dynamic_slice_in_dim(labels, first_row + reach_rows, block_rows, 0)
        key_labels = lax.dynamic_slice_in_dim(labels, first_row, window, 0)
        scores = (
            jnp.einsum("hdq,hdk->hqk", queries, key_block, preferred_element_type=jnp.float32)
            * score_scale
        )
        same_image = (query_labels[:, None] == key_labels[None, :])[None]
        scores = jnp.where(same_image, scores, -1e30)
        row_max = jnp.max(scores, axis=2, keepdims=True)
        exponent = jnp.exp(scores - row_max)
        totals = jnp.sum(exponent, axis=2)
        weights = exponent.astype(jnp.bfloat16)
        weighted = jnp.einsum(
            "hqk,hdk->hdq", weights, value_block, preferred_element_type=jnp.float32
        )
        weighted = weighted / totals[:, None, :]
        return weighted.astype(jnp.bfloat16).reshape(width_here, block_rows)

    attended = lax.map(attend, jnp.arange(block_count, dtype=jnp.int32))
    attended = jnp.transpose(attended, (1, 0, 2)).reshape(width_here, tok_rows)
    head_weight = lax.dynamic_slice_in_dim(out_weight, col_id * width_here, width_here, 0)
    partial_value = lax.dot_general(
        head_weight, attended, (((0,), (0,)), ((), ())), preferred_element_type=jnp.float32
    )
    projected = lax.psum_scatter(partial_value, "col", scatter_dimension=0, tiled=True)
    layer_out = (residual_in.astype(jnp.float32) + projected).astype(jnp.bfloat16)
    full_rows = lax.all_gather(layer_out, "col", axis=0, tiled=True)
    values32 = full_rows.astype(jnp.float32)
    centre = jnp.mean(values32, axis=0, keepdims=True)
    spread = jnp.mean(jnp.square(values32 - centre), axis=0, keepdims=True)
    normed = ((values32 - centre) * lax.rsqrt(spread + 1e-06) * merge_gain[:, None]).astype(
        jnp.bfloat16
    )
    group_rows = tok_rows // 4
    grouped = normed.reshape(full_width, group_rows, 4)
    weight_parts = merge_weight.reshape(width_here, 4, full_width)
    merged = jnp.einsum(
        "ojf,fgj->og", weight_parts, grouped, preferred_element_type=jnp.float32
    ).astype(jnp.bfloat16)
    empty_rows = jnp.zeros((width_here, group_rows), jnp.bfloat16)
    every_row, every_dest = (
        lax.all_gather(merged, "row", axis=1, tiled=True),
        lax.all_gather(dest_row, "row", axis=0, tiled=True),
    )
    slot_index = every_dest - row_id * group_rows
    slot_index = jnp.where((slot_index >= 0) & (slot_index < group_rows), slot_index, group_rows)
    image_rows = empty_rows.at[:, slot_index].set(every_row, mode="drop")
    return (layer_out, image_rows)


def solution(mesh):
    return jax.shard_map(
        body,
        mesh=mesh,
        in_specs=(P(None, "col", "row"), P("col", "row"), P(), P("col", None), P(), P(), P("row")),
        out_specs=(P("col", "row"), P("col", "row")),
        check_vma=False,
    )
```

profile of v0, /device:TPU:0, one launch (start us, length us, event | category | flops | bytes accessed | tf_op | source)
XLA Modules:
  0.0 381.6 jit_solution(7010875313808431647)
XLA Ops:
  7.2 2.4 fusion.44
  9.7 3.9 %collective-permute-start = (bf16[2,176,1024]{2,1,0:T(8,128)(2,1)}, bf16[2,176,1024]{2,1,0:T(8,128)(2,1)S(1)}, u32[]{:S(2)}, u32[]{:S(2)}) collective-permute-start(bf16[2,176,1024]{2,1,0:T(8,128)(2,1)} %get-tuple-element.106), channel_id=1, source_target_pairs={{0,8},{8,16},{16,24},{24,32},{32,40},{40,48},{48,56},{56,64},{64,7... | collective-permute-start | bytes 2162696 | tf_op jit(solution)/shard_map/ppermute | solution.py:18
  13.6 1.3 collective-permute-start.1
  15.0 0.1 copy.28
  15.1 0.1 reduce-window.8
  15.2 0.1 multiply_reduce_fusion
  15.3 0.2 convert_reduce_fusion.1
  15.5 13.8 %collective-permute-done = bf16[2,176,1024]{2,1,0:T(8,128)(2,1)S(1)} collective-permute-done((bf16[2,176,1024]{2,1,0:T(8,128)(2,1)}, bf16[2,176,1024]{2,1,0:T(8,128)(2,1)S(1)}, u32[]{:S(2)}, u32[]{:S(2)}) %collective-permute-start) | collective-permute-done | bytes 720928 | tf_op jit(solution)/shard_map/ppermute | solution.py:18
  29.3 4.1 %collective-permute-done.1 = bf16[2,176,1024]{2,1,0:T(8,128)(2,1)} collective-permute-done((bf16[2,176,1024]{2,1,0:T(8,128)(2,1)S(1)}, bf16[2,176,1024]{2,1,0:T(8,128)(2,1)}, u32[]{:S(2)}, u32[]{:S(2)}) %collective-permute-start.1) | collective-permute-done | bytes 720928 | tf_op jit(solution)/shard_map/ppermute | solution.py:20
  33.4 3.1 pad_maximum_fusion
  36.4 91.2 %while.12 = (s32[]{:T(128)}, bf16[2,176,1024]{2,1,0:T(8,128)(2,1)}, bf16[2,176,4096]{2,1,0:T(8,128)(2,1)}, s32[2]{0:T(128)S(1)}, s32[4096]{0:T(1024)S(1)}, /*ind...) while((s32[]{:T(128)}, bf16[2,176,1024]{2,1,0:T(8,128)(2,1)}, ...), condition=%wide.region_5.6_spmd, body=%wide.region_2.5_spmd.sunk | while | flops 2287300608 | bytes 108356392 | solution.py:83
  36.4 0.7 dynamic_slice.44
  37.8 2.0 broadcast_compare_fusion.2
  39.8 2.1 fusion.61
  41.9 1.6 constant_dynamic-slice_fusion.5
  43.6 1.2 slice.41
  44.8 12.6 %fusion.62 = (f32[2,1024]{1,0:T(2,128)S(1)}, f32[2,1024,3072]{2,1,0:T(8,128)}) fusion(pred[1024,3072]{1,0:T(8,128)(4,1)S(1)} %broadcast_compare_fusion.2, bf16[2,88,1024]{2,1,0:T(8,128)(2,1)S(1)} %bitcast.59, bf16[2,88,3072]{2,1,0:T(8,128)(2,1)} %bitcast.57), kind=kOutput, calls=%fused_computation.3.clone.1 | convolution fusion | flops 1126168576 | bytes 29761536 | tf_op jit(solution)/shard_map/while/body/eval_jaxpr/hdq,hdk->hqk/dot_general | solution.py:68
  57.4 12.0 %fusion.63 = f32[2,1024]{1,0:T(2,128)S(1)} fusion(f32[2,1024,3072]{2,1,0:T(8,128)} %get-tuple-element.155, f32[2,1024]{1,0:T(2,128)S(1)} %get-tuple-element.156, pred[1024,3072]{1,0:T(8,128)(4,1)S(1)} %broadcast_compare_fusion.2), kind=kLoop, calls=%fused_computation.4.clone.1 | loop fusion | flops 25163776 | bytes 28327936 | tf_op jit(solution)/shard_map/while/body/eval_jaxpr/reduce_sum | solution.py:75
  69.4 11.8 %fusion.64 = bf16[2,88,1024]{2,1,0:T(8,128)(2,1)S(1)} fusion(bf16[2,88,3072]{2,1,0:T(8,128)(2,1)S(1)} %bitcast.56, f32[2,1024,3072]{2,1,0:T(8,128)} %get-tuple-element.155, f32[2,1024]{1,0:T(2,128)S(1)} %get-tuple-element.156, pred[1024,3072]{1,0:T(8,128)(4,1)S(1)} %broadcast_compare_fusion.2, f32[2,1024]{1,0:T(2,128)S(1)} %fusion.63), kind=kOutput, calls=%fused_computation.10.clone.1 | convolution fusion | flops 1132822528 | bytes 29769728 | tf_op jit(solution)/shard_map/while/body/eval_jaxpr/hqk,hdk->hdq/dot_general | solution.py:77
  81.3 0.8 bitcast_dynamic-update-slice_fusion.2
  82.0 0.7 dynamic_slice.44
  83.4 2.0 broadcast_compare_fusion.2
  85.4 2.1 fusion.61
  87.5 1.6 constant_dynamic-slice_fusion.5
  89.2 1.2 slice.41
  90.4 12.6 %fusion.62 = (f32[2,1024]{1,0:T(2,128)S(1)}, f32[2,1024,3072]{2,1,0:T(8,128)}) fusion(pred[1024,3072]{1,0:T(8,128)(4,1)S(1)} %broadcast_compare_fusion.2, bf16[2,88,1024]{2,1,0:T(8,128)(2,1)S(1)} %bitcast.59, bf16[2,88,3072]{2,1,0:T(8,128)(2,1)} %bitcast.57), kind=kOutput, calls=%fused_computation.3.clone.1 | convolution fusion | flops 1126168576 | bytes 29761536 | tf_op jit(solution)/shard_map/while/body/eval_jaxpr/hdq,hdk->hqk/dot_general | solution.py:68
  103.0 12.0 %fusion.63 = f32[2,1024]{1,0:T(2,128)S(1)} fusion(f32[2,1024,3072]{2,1,0:T(8,128)} %get-tuple-element.155, f32[2,1024]{1,0:T(2,128)S(1)} %get-tuple-element.156, pred[1024,3072]{1,0:T(8,128)(4,1)S(1)} %broadcast_compare_fusion.2), kind=kLoop, calls=%fused_computation.4.clone.1 | loop fusion | flops 25163776 | bytes 28327936 | tf_op jit(solution)/shard_map/while/body/eval_jaxpr/reduce_sum | solution.py:75
  115.0 11.8 %fusion.64 = bf16[2,88,1024]{2,1,0:T(8,128)(2,1)S(1)} fusion(bf16[2,88,3072]{2,1,0:T(8,128)(2,1)S(1)} %bitcast.56, f32[2,1024,3072]{2,1,0:T(8,128)} %get-tuple-element.155, f32[2,1024]{1,0:T(2,128)S(1)} %get-tuple-element.156, pred[1024,3072]{1,0:T(8,128)(4,1)S(1)} %broadcast_compare_fusion.2, f32[2,1024]{1,0:T(2,128)S(1)} %fusion.63), kind=kOutput, calls=%fused_computation.10.clone.1 | convolution fusion | flops 1132822528 | bytes 29769728 | tf_op jit(solution)/shard_map/while/body/eval_jaxpr/hqk,hdk->hdq/dot_general | solution.py:77
  126.9 0.8 bitcast_dynamic-update-slice_fusion.2
  127.7 1.2 copy.36
  128.8 7.1 %fusion.38 = f32[1408,2048]{1,0:T(8,128)} fusion(bf16[176,2048]{1,0:T(8,128)(2,1)S(1)} %bitcast.61, bf16[1408,1408]{1,0:T(8,128)(2,1)} %param.11, s32[]{:T(128)S(6)} %select_n.41), kind=kOutput, calls=%fused_computation.34 | convolution fusion | flops 1015021568 | bytes 12750852 | tf_op jit(solution)/shard_map/dot_general | solution.py:86
  135.9 0.2 all-gather.4.cloned.1.call-start
  136.2 70.0 %reduce-scatter.2.cloned.1.call-done = f32[176,2048]{1,0:T(8,128)} async-done(((f32[1408,2048]{1,0:T(8,128)}), f32[176,2048]{1,0:T(8,128)}) %reduce-scatter.2.cloned.1.call-update) | async-done | bytes 1441808 | tf_op jit(solution)/shard_map/reduce_scatter | solution.py:89
  206.2 2.4 add_convert_fusion
  208.6 0.0 all-gather.6.cloned.1.call-start
  208.7 38.4 %all-gather.4.cloned.1.call-done = bf16[1408,2048]{1,0:T(8,128)(2,1)} async-done(((bf16[176,2048]{1,0:T(8,128)(2,1)}), bf16[1408,2048]{1,0:T(8,128)(2,1)}) %all-gather.4.cloned.1.call-update) | async-done | bytes 5767184 | tf_op jit(solution)/shard_map/all_gather | solution.py:91
  247.1 3.7 convert_reduce_fusion
  250.8 0.6 copy-done
  251.4 1.5 fusion.16
  253.0 4.3 %fusion.18 = bf16[1408,2048]{1,0:T(8,128)(2,1)} fusion(bf16[1408,2048]{1,0:T(8,128)(2,1)S(1)} %copy-done, f32[1408]{0:T(1024)S(1)} %copy-done.3, f32[2048]{0:T(1024)S(1)} %add_rsqrt_fusion, f32[2048]{0:T(1024)S(1)} %broadcast_multiply_fusion), kind=kLoop, calls=%fused_computation.23 | loop fusion | flops 14417920 | bytes 11556352 | tf_op jit(solution)/shard_map/convert_element_type | solution.py:95
  257.2 8.4 %copy.30 = bf16[1408,2048]{0,1:T(8,128)(2,1)} copy(bf16[1408,2048]{1,0:T(8,128)(2,1)} %fusion.18) | data formatting | bytes 11534336 | tf_op jit(solution)/shard_map/convert_element_type | solution.py:95
  265.6 10.6 %reshape.116 = bf16[1408,512,4]{0,2,1:T(4,128)(2,1)} reshape(bf16[1408,2048]{0,1:T(8,128)(2,1)} %copy.30) | data formatting | bytes 11534336 | tf_op jit(solution)/shard_map/reshape | solution.py:99
  276.2 5.4 %fusion.33 = bf16[176,512]{1,0:T(8,128)(2,1)} fusion(bf16[1408,512,4]{0,2,1:T(4,128)(2,1)} %reshape.116, bf16[22,4,8,1408]{3,2,1,0:T(8,128)(2,1)S(1)} %bitcast.67), kind=kOutput, calls=%fused_computation.32 | convolution fusion | flops 1015111680 | bytes 7929856 | tf_op jit(solution)/shard_map/ojf,fgj->og/dot_general | solution.py:101
  281.7 23.5 %all-gather = s32[16,1,512]{2,1,0:T(1,128)S(1)} all-gather(s32[1,1,512]{2,1,0:T(1,128)S(1)} %bitcast.65), channel_id=1, replica_groups=mesh['row'=16,'col'=8] {'row'}, dimensions={0}, use_global_device_ids=true | all-gather | bytes 34816 | tf_op jit(solution)/shard_map/all_gather | solution.py:107
  305.2 28.1 %all-gather.6.cloned.1.call-done = bf16[176,8192]{1,0:T(8,128)(2,1)} async-done(((bf16[176,512]{1,0:T(8,128)(2,1)}), bf16[176,8192]{1,0:T(8,128)(2,1)}) %all-gather.6.cloned.1.call-update) | async-done | bytes 2883600 | tf_op jit(solution)/shard_map/all_gather | solution.py:106
  333.3 5.8 %copy.33 = bf16[8192,176]{1,0:T(8,128)(2,1)} copy(bf16[8192,176]{0,1:T(8,128)(2,1)} %bitcast.60) | data formatting | bytes 5767168 | tf_op jit(solution)/shard_map/all_gather | solution.py:106
  339.1 35.2 %scatter_custom_fusion = bf16[176,512]{0,1:T(8,128)(2,1)S(1)} fusion(s32[8192]{0:T(1024)S(1)} %compare_select_fusion, bf16[8192,176]{1,0:T(8,128)(2,1)} %copy.33, bf16[]{:T(256)} %constant.97.clone.1), kind=kCustom, calls=%fused_computation.36 | custom fusion | bytes 180736 | tf_op jit(solution)/shard_map/scatter | solution.py:111
  374.3 0.8 copy.34
  (35 shorter events, 0.3 us)
Async XLA Ops:
  7.2 26.2 %slice-start = ((bf16[3,176,2048]{2,1,0:T(8,128)(2,1)}), bf16[2,176,2048]{2,1,0:T(8,128)(2,1)S(1)}, s32[]{:S(2)}) async-start(bf16[3,176,2048]{2,1,0:T(8,128)(2,1)} %param.9), calls=%async_computation.4 | async-start | bytes 2883584 | tf_op jit(solution)/shard_map/slice | solution.py:48
  7.2 7.8 %copy-start.5 = (s32[64]{0:T(128)S(1)}, s32[64]{0:T(128)}, u32[]{:S(2)}) copy-start(s32[64]{0:T(128)} %param.14) | copy-start | bytes 772
  7.2 199.0 %reduce-scatter.2.cloned.1.call-start = ((), (), s32[]{:S(2)}) async-start(), calls=%async_computation.1 | async-start | bytes 12976128 | tf_op jit(solution)/shard_map/reduce_scatter | solution.py:89
  9.7 19.6 %collective-permute-start = (bf16[2,176,1024]{2,1,0:T(8,128)(2,1)}, bf16[2,176,1024]{2,1,0:T(8,128)(2,1)S(1)}, u32[]{:S(2)}, u32[]{:S(2)}) collective-permute-start(bf16[2,176,1024]{2,1,0:T(8,128)(2,1)} %get-tuple-element.106), channel_id=1, source_target_pairs={{0,8},{8,16},{16,24},{24,32},{32,40},{40,48},{48,56},{56,64},{64,7... | collective-permute-start | bytes 2162696 | tf_op jit(solution)/shard_map/ppermute | solution.py:18
  13.6 19.7 %collective-permute-start.1 = (bf16[2,176,1024]{2,1,0:T(8,128)(2,1)S(1)}, bf16[2,176,1024]{2,1,0:T(8,128)(2,1)}, u32[]{:S(2)}, u32[]{:S(2)}) collective-permute-start(bf16[2,176,1024]{2,1,0:T(8,128)(2,1)S(1)} %get-tuple-element.107), channel_id=1, source_target_pairs={{8,0},{16,8},{24,16},{32,24},{40,32},{48,40},{56,48},{64,56},{72,6... | collective-permute-start | bytes 2162696 | tf_op jit(solution)/shard_map/ppermute | solution.py:20
  57.4 12.0 %copy-start.1 = (bf16[1,176,3072]{2,1,0:T(8,128)(2,1)S(1)}, bf16[1,176,3072]{2,1,0:T(8,128)(2,1)}, u32[]{:S(2)}) copy-start(bf16[1,176,3072]{2,1,0:T(8,128)(2,1)} %get-tuple-element.153) | copy-start | bytes 3244036 | tf_op jit(solution)/shard_map/while
  103.0 12.0 %copy-start.1 = (bf16[1,176,3072]{2,1,0:T(8,128)(2,1)S(1)}, bf16[1,176,3072]{2,1,0:T(8,128)(2,1)}, u32[]{:S(2)}) copy-start(bf16[1,176,3072]{2,1,0:T(8,128)(2,1)} %get-tuple-element.153) | copy-start | bytes 3244036 | tf_op jit(solution)/shard_map/while
  135.9 70.3 %copy-start.2 = (bf16[176,2048]{1,0:T(8,128)(2,1)S(1)}, bf16[176,2048]{1,0:T(8,128)(2,1)}, u32[]{:S(2)}) copy-start(bf16[176,2048]{1,0:T(8,128)(2,1)} %param.10) | copy-start | bytes 2162692
  135.9 111.1 %all-gather.4.cloned.1.call-start = ((), (), s32[]{:S(2)}) async-start(), calls=%async_computation.2 | async-start | bytes 6488064 | tf_op jit(solution)/shard_map/all_gather | solution.py:91
  208.6 44.3 %copy-start.3 = (f32[1408]{0:T(1024)S(1)}, f32[1408]{0:T(1024)}, u32[]{:S(2)}) copy-start(f32[1408]{0:T(1024)} %param.13) | copy-start | bytes 16900
  208.6 124.7 %all-gather.6.cloned.1.call-start = ((), (), s32[]{:S(2)}) async-start(), calls=%async_computation.3 | async-start | bytes 3063808 | tf_op jit(solution)/shard_map/all_gather | solution.py:106
  247.1 4.3 %copy-start = (bf16[1408,2048]{1,0:T(8,128)(2,1)S(1)}, bf16[1408,2048]{1,0:T(8,128)(2,1)}, u32[]{:S(2)}) copy-start(bf16[1408,2048]{1,0:T(8,128)(2,1)} %all-gather.4.cloned.1.call-done) | copy-start | bytes 17301508
  265.6 10.7 %copy-start.6 = (bf16[176,5632]{1,0:T(8,128)(2,1)S(1)}, bf16[176,5632]{1,0:T(8,128)(2,1)}, u32[]{:S(2)}) copy-start(bf16[176,5632]{1,0:T(8,128)(2,1)} %param.12) | copy-start | bytes 5947396
  276.2 5.4 %copy-start.4 = (s32[512]{0:T(512)S(1)}, s32[512]{0:T(512)}, u32[]{:S(2)}) copy-start(s32[512]{0:T(512)} %param.15) | copy-start | bytes 6148
Sparse Core Ops, SparseCore 0:
  136.1 70.0 reduce-scatter.1
  208.7 38.2 all-gather.3
  281.8 51.4 all-gather.5
where the time goes:
time: 383 us; the launch traced here: 382 us
  waiting for transfers between devices  154 us (40%)
  local copies, waits for them, and re-layouts  77.9 us (20%)
  matrix products  61.4 us (16%)
  other arithmetic  43.4 us (11%)
  blocking collectives  23.5 us (6%)
  between operations  13.9 us (4%)
  starting transfers between devices  5.53 us (1%)
    reduce_scatter x1, waiting for transfers between devices, body(): lax.psum_scatter(partial_value, 'col', scatter_dimension=0, tiled=True)  70 us
    all_gather x1, waiting for transfers between devices, body(): full_rows = lax.all_gather(layer_out, 'col', axis=0, tiled=True)  38.4 us
    scatter x1, local copies, waits for them, and re-layouts, body(): image_rows = empty_rows.at[:, slot_index].set(every_row, mode='drop')  35.2 us
    all_gather x1, waiting for transfers between devices, body(): lax.all_gather(merged, 'row', axis=1, tiled=True)  28.1 us
    dot_general x2, matrix products, attend(): jnp.einsum('hdq,hdk->hqk', queries, key_block, preferred_element_type=jnp...  25.3 us
    reduce_sum x2, other arithmetic, attend(): totals = jnp.sum(exponent, axis=2)  24 us
    dot_general x2, matrix products, attend(): jnp.einsum('hqk,hdk->hdq', weights, value_block, preferred_element_type=j...  23.7 us
    all_gather x1, blocking collectives, body(): lax.all_gather(dest_row, 'row', axis=0, tiled=True)  23.5 us
  transfers between devices with their start and end apart: 5, of which 5 were waited for; matrix products, arithmetic and copies ran while one was open for 0% of the time, Pallas kernels for 0%

commit v1 on v0

--- a/solution.py
+++ b/solution.py
@@ -88,7 +88,33 @@
     )
     projected = lax.psum_scatter(partial_value, "col", scatter_dimension=0, tiled=True)
     layer_out = (residual_in.astype(jnp.float32) + projected).astype(jnp.bfloat16)
-    full_rows = lax.all_gather(layer_out, "col", axis=0, tiled=True)
+    mixed_arr, before, kept_arr = (
+        jax.lax.axis_size("col"),
+        jax.lax.axis_index("col"),
+        layer_out.shape[0],
+    )
+    log = []
+    for q in range(mixed_arr):
+        log.append((q, (q + 1) % mixed_arr))
+    by_rank = []
+    for q in range(mixed_arr):
+        by_rank.append((q, (q - 1) % mixed_arr))
+    full_rows = jnp.zeros(
+        (*layer_out.shape[:0], mixed_arr * kept_arr, *layer_out.shape[1:]), layer_out.dtype
+    )
+    piece_out = reached = layer_out
+    extra = mixed_arr // 2
+    full_rows = lax.dynamic_update_slice_in_dim(full_rows, layer_out, before * kept_arr, axis=0)
+    for d in range(1, extra + 1):
+        piece_out = jax.lax.ppermute(piece_out, axis_name="col", perm=log)
+        full_rows = lax.dynamic_update_slice_in_dim(
+            full_rows, piece_out, (before - d) % mixed_arr * kept_arr, axis=0
+        )
+        if d < mixed_arr - extra:
+            reached = jax.lax.ppermute(reached, axis_name="col", perm=by_rank)
+            full_rows = lax.dynamic_update_slice_in_dim(
+                full_rows, reached, (before + d) % mixed_arr * kept_arr, axis=0
+            )
     values32 = full_rows.astype(jnp.float32)
     centre = jnp.mean(values32, axis=0, keepdims=True)
     spread = jnp.mean(jnp.square(values32 - centre), axis=0, keepdims=True)

time: 383 us -> 479 us (1.25)
  local copies, waits for them, and re-layouts: 77.9 us -> 174 us
  waiting for transfers between devices: 154 us -> 143 us
  starting transfers between devices: 5.53 us -> 15.8 us
    dynamic_update_slice x0 -> x8, local copies, waits for them, and re-layouts: none -> 89.2 us  [the longest x4 44.7 us: body(): lax.dynamic_update_slice_in_dim(full_rows, piece_out, (before - d) % mixe...]
    all_gather x1 -> x0, waiting for transfers between devices: 38.4 us -> none  [body(): full_rows = lax.all_gather(layer_out, 'col', axis=0, tiled=True)]
    ppermute x0 -> x7, waiting for transfers between devices: none -> 26.9 us  [the longest x4 26.9 us: body(): piece_out = jax.lax.ppermute(piece_out, axis_name='col', perm=log)]
    ppermute x1, waiting for transfers between devices: 13.8 us -> 0.97 us  [with_halo(): lax.ppermute(tail, axis, [(i, (i + 1) % count) for i in range(ends)])]
    ppermute x1, waiting for transfers between devices: 4.09 us -> 13 us  [with_halo(): lax.ppermute(head, axis, [((i + 1) % count, i) for i in range(ends)])]
    ppermute x0 -> x7, starting transfers between devices: none -> 8.86 us  [the longest x3 8.84 us: body(): reached = jax.lax.ppermute(reached, axis_name='col', perm=by_rank)]
    ppermute x0 -> x7, local copies, waits for them, and re-layouts: none -> 8.09 us  [the longest x4 4.75 us: body(): piece_out = jax.lax.ppermute(piece_out, axis_name='col', perm=log)]
    convert_element_type x1, local copies, waits for them, and re-layouts: 8.37 us -> 0.51 us  [body(): (residual_in.astype(jnp.float32) + projected).astype(jnp.bfloat16)]
  transfers between devices with their start and end apart: 5 -> 11, of which waited for: 5 -> 7; matrix products, arithmetic and copies ran while one was open for 0% -> 19% of each run, Pallas kernels for 0% -> 0%
where the time goes in v1:
time: 479 us; the launch traced here: 475 us
  local copies, waits for them, and re-layouts  174 us (36%)
  waiting for transfers between devices  143 us (30%)
  matrix products  61.4 us (13%)
  other arithmetic  42.2 us (9%)
  blocking collectives  23.7 us (5%)
  starting transfers between devices  15.8 us (3%)
  between operations  14.4 us (3%)
    reduce_scatter x1, waiting for transfers between devices, body(): lax.psum_scatter(partial_value, 'col', scatter_dimension=0, tiled=True)  72.8 us
    dynamic_update_slice x4, local copies, waits for them, and re-layouts, body(): lax.dynamic_update_slice_in_dim(full_rows, piece_out, (before - d) % mixe...  44.7 us
    scatter x1, local copies, waits for them, and re-layouts, body(): image_rows = empty_rows.at[:, slot_index].set(every_row, mode='drop')  35.2 us
    dynamic_update_slice x3, local copies, waits for them, and re-layouts, body(): lax.dynamic_update_slice_in_dim(full_rows, reached, (before + d) % mixed_...  34.3 us
    all_gather x1, waiting for transfers between devices, body(): lax.all_gather(merged, 'row', axis=1, tiled=True)  29 us
    ppermute x4, waiting for transfers between devices, body(): piece_out = jax.lax.ppermute(piece_out, axis_name='col', perm=log)  26.9 us
    dot_general x2, matrix products, attend(): jnp.einsum('hdq,hdk->hqk', queries, key_block, preferred_element_type=jnp...  25.2 us
    reduce_sum x2, other arithmetic, attend(): totals = jnp.sum(exponent, axis=2)  24 us
  transfers between devices with their start and end apart: 11, of which 7 were waited for; matrix products, arithmetic and copies ran while one was open for 19% of the time, Pallas kernels for 0%

profile of v1, /device:TPU:0, one launch (start us, length us, event | category | flops | bytes accessed | tf_op | source)
XLA Modules:
  0.0 475.1 jit_solution(13865369379133073010)
XLA Ops:
  7.2 2.5 fusion.44
  11.0 5.4 %collective-permute-start = (bf16[2,176,1024]{2,1,0:T(8,128)(2,1)S(1)}, bf16[2,176,1024]{2,1,0:T(8,128)(2,1)}, u32[]{:S(2)}, u32[]{:S(2)}) collective-permute-start(bf16[2,176,1024]{2,1,0:T(8,128)(2,1)S(1)} %get-tuple-element.106), channel_id=1, source_target_pairs={{0,8},{8,16},{16,24},{24,32},{32,40},{40,48},{48,56},{56,64},{64,7... | collective-permute-start | bytes 2162696 | tf_op jit(solution)/shard_map/ppermute | solution.py:18
  17.0 13.0 %collective-permute-done.1 = bf16[2,176,1024]{2,1,0:T(8,128)(2,1)S(1)} collective-permute-done((bf16[2,176,1024]{2,1,0:T(8,128)(2,1)}, bf16[2,176,1024]{2,1,0:T(8,128)(2,1)S(1)}, u32[]{:S(2)}, u32[]{:S(2)}) %collective-permute-start.1) | collective-permute-done | bytes 720928 | tf_op jit(solution)/shard_map/ppermute | solution.py:20
  30.9 3.0 pad_maximum_fusion
  34.0 94.3 %while.12 = (s32[]{:T(128)}, bf16[2,176,1024]{2,1,0:T(8,128)(2,1)}, bf16[2,176,4096]{2,1,0:T(8,128)(2,1)}, s32[2]{0:T(128)S(1)}, s32[4096]{0:T(1024)S(1)}, /*ind...) while((s32[]{:T(128)}, bf16[2,176,1024]{2,1,0:T(8,128)(2,1)}, ...), condition=%wide.region_5.6_spmd, body=%wide.region_2.5_spmd.sunk | while | flops 2287300608 | bytes 108355888 | solution.py:83
  34.0 2.0 fusion.61
  37.2 1.6 constant_dynamic-slice_fusion.5
  38.8 2.0 broadcast_compare_fusion.2
  40.8 2.0 slice.41
  43.9 12.6 %fusion.62 = (f32[2,1024]{1,0:T(2,128)S(1)}, f32[2,1024,3072]{2,1,0:T(8,128)}) fusion(pred[1024,3072]{1,0:T(8,128)(4,1)S(1)} %broadcast_compare_fusion.2, bf16[2,88,1024]{2,1,0:T(8,128)(2,1)S(1)} %bitcast.59, bf16[2,88,3072]{2,1,0:T(8,128)(2,1)} %bitcast.57), kind=kOutput, calls=%fused_computation.3.clone.1 | convolution fusion | flops 1126168576 | bytes 29761536 | tf_op jit(solution)/shard_map/while/body/eval_jaxpr/hdq,hdk->hqk/dot_general | solution.py:68
  56.5 12.0 %fusion.63 = f32[2,1024]{1,0:T(2,128)S(1)} fusion(f32[2,1024,3072]{2,1,0:T(8,128)} %get-tuple-element.155, f32[2,1024]{1,0:T(2,128)S(1)} %get-tuple-element.156, pred[1024,3072]{1,0:T(8,128)(4,1)S(1)} %broadcast_compare_fusion.2), kind=kLoop, calls=%fused_computation.4.clone.1 | loop fusion | flops 25163776 | bytes 28327936 | tf_op jit(solution)/shard_map/while/body/eval_jaxpr/reduce_sum | solution.py:75
  68.5 11.8 %fusion.64 = bf16[2,88,1024]{2,1,0:T(8,128)(2,1)S(1)} fusion(bf16[2,88,3072]{2,1,0:T(8,128)(2,1)S(1)} %bitcast.56, f32[2,1024,3072]{2,1,0:T(8,128)} %get-tuple-element.155, f32[2,1024]{1,0:T(2,128)S(1)} %get-tuple-element.156, pred[1024,3072]{1,0:T(8,128)(4,1)S(1)} %broadcast_compare_fusion.2, f32[2,1024]{1,0:T(2,128)S(1)} %fusion.63), kind=kOutput, calls=%fused_computation.10.clone.1 | convolution fusion | flops 1132822528 | bytes 29769728 | tf_op jit(solution)/shard_map/while/body/eval_jaxpr/hqk,hdk->hdq/dot_general | solution.py:77
  81.1 2.0 fusion.61
  84.3 1.6 constant_dynamic-slice_fusion.5
  86.0 2.0 broadcast_compare_fusion.2
  87.9 2.0 slice.41
  91.0 12.6 %fusion.62 = (f32[2,1024]{1,0:T(2,128)S(1)}, f32[2,1024,3072]{2,1,0:T(8,128)}) fusion(pred[1024,3072]{1,0:T(8,128)(4,1)S(1)} %broadcast_compare_fusion.2, bf16[2,88,1024]{2,1,0:T(8,128)(2,1)S(1)} %bitcast.59, bf16[2,88,3072]{2,1,0:T(8,128)(2,1)} %bitcast.57), kind=kOutput, calls=%fused_computation.3.clone.1 | convolution fusion | flops 1126168576 | bytes 29761536 | tf_op jit(solution)/shard_map/while/body/eval_jaxpr/hdq,hdk->hqk/dot_general | solution.py:68
  103.6 12.0 %fusion.63 = f32[2,1024]{1,0:T(2,128)S(1)} fusion(f32[2,1024,3072]{2,1,0:T(8,128)} %get-tuple-element.155, f32[2,1024]{1,0:T(2,128)S(1)} %get-tuple-element.156, pred[1024,3072]{1,0:T(8,128)(4,1)S(1)} %broadcast_compare_fusion.2), kind=kLoop, calls=%fused_computation.4.clone.1 | loop fusion | flops 25163776 | bytes 28327936 | tf_op jit(solution)/shard_map/while/body/eval_jaxpr/reduce_sum | solution.py:75
  115.6 11.8 %fusion.64 = bf16[2,88,1024]{2,1,0:T(8,128)(2,1)S(1)} fusion(bf16[2,88,3072]{2,1,0:T(8,128)(2,1)S(1)} %bitcast.56, f32[2,1024,3072]{2,1,0:T(8,128)} %get-tuple-element.155, f32[2,1024]{1,0:T(2,128)S(1)} %get-tuple-element.156, pred[1024,3072]{1,0:T(8,128)(4,1)S(1)} %broadcast_compare_fusion.2, f32[2,1024]{1,0:T(2,128)S(1)} %fusion.63), kind=kOutput, calls=%fused_computation.10.clone.1 | convolution fusion | flops 1132822528 | bytes 29769728 | tf_op jit(solution)/shard_map/while/body/eval_jaxpr/hqk,hdk->hdq/dot_general | solution.py:77
  129.4 7.1 %fusion.38 = f32[1408,2048]{1,0:T(8,128)} fusion(bf16[176,2048]{1,0:T(8,128)(2,1)S(1)} %bitcast.61, bf16[1408,1408]{1,0:T(8,128)(2,1)} %param.11, s32[]{:T(128)S(6)} %select_n.94), kind=kOutput, calls=%fused_computation.34 | convolution fusion | flops 1015021568 | bytes 12750852 | tf_op jit(solution)/shard_map/dot_general | solution.py:86
  136.8 72.8 %reduce-scatter.2.cloned.1.call-done = f32[176,2048]{1,0:T(8,128)} async-done(((f32[1408,2048]{1,0:T(8,128)}), f32[176,2048]{1,0:T(8,128)}) %reduce-scatter.2.cloned.1.call-update) | async-done | bytes 1441808 | tf_op jit(solution)/shard_map/reduce_scatter | solution.py:89
  209.5 1.5 add_convert_fusion
  211.1 2.9 collective-permute-start.3
  214.1 9.0 %collective-permute-done.2 = bf16[176,2048]{1,0:T(8,128)(2,1)S(1)} collective-permute-done((bf16[176,2048]{1,0:T(8,128)(2,1)S(1)}, bf16[176,2048]{1,0:T(8,128)(2,1)S(1)}, u32[]{:S(2)}, u32[]{:S(2)}) %collective-permute-start.2) | collective-permute-done | bytes 720928 | tf_op jit(solution)/shard_map/ppermute | solution.py:109
  223.0 2.9 collective-permute-start.5
  226.0 9.0 %collective-permute-done.4 = bf16[176,2048]{1,0:T(8,128)(2,1)S(1)} collective-permute-done((bf16[176,2048]{1,0:T(8,128)(2,1)S(1)}, bf16[176,2048]{1,0:T(8,128)(2,1)S(1)}, u32[]{:S(2)}, u32[]{:S(2)}) %collective-permute-start.4) | collective-permute-done | bytes 720928 | tf_op jit(solution)/shard_map/ppermute | solution.py:109
  235.0 3.0 collective-permute-start.7
  237.9 9.0 %collective-permute-done.6 = bf16[176,2048]{1,0:T(8,128)(2,1)S(1)} collective-permute-done((bf16[176,2048]{1,0:T(8,128)(2,1)S(1)}, bf16[176,2048]{1,0:T(8,128)(2,1)S(1)}, u32[]{:S(2)}, u32[]{:S(2)}) %collective-permute-start.6) | collective-permute-done | bytes 720928 | tf_op jit(solution)/shard_map/ppermute | solution.py:109
  247.5 2.9 broadcast_in_dim.58
  250.4 10.2 %dynamic_update_slice.31 = bf16[1408,2048]{0,1:T(8,128)(2,1)} dynamic-update-slice(bf16[1408,2048]{0,1:T(8,128)(2,1)} %broadcast_in_dim.58, bf16[176,2048]{0,1:T(8,128)(2,1)S(1)} %copy.43, s32[]{:T(128)S(6)} %select_n.94, s32[]{:T(128)} %constant.138.clone.1) | dynamic-update-slice | bytes 1441796 | tf_op jit(solution)/shard_map/dynamic_update_slice | solution.py:107
  262.1 10.7 %dynamic_update_slice.32 = bf16[1408,2048]{0,1:T(8,128)(2,1)} dynamic-update-slice(bf16[1408,2048]{0,1:T(8,128)(2,1)} %dynamic_update_slice.31, bf16[176,2048]{0,1:T(8,128)(2,1)S(1)} %copy.44, s32[]{:T(128)S(6)} %select_n.99, s32[]{:T(128)} %constant.138.clone.1) | dynamic-update-slice | bytes 1441796 | tf_op jit(solution)/shard_map/dynamic_update_slice | solution.py:110
  274.2 11.5 %dynamic_update_slice.33 = bf16[1408,2048]{0,1:T(8,128)(2,1)} dynamic-update-slice(bf16[1408,2048]{0,1:T(8,128)(2,1)} %dynamic_update_slice.32, bf16[176,2048]{0,1:T(8,128)(2,1)S(1)} %copy.45, s32[]{:T(128)S(6)} %select_n.101, s32[]{:T(128)} %constant.138.clone.1) | dynamic-update-slice | bytes 1441796 | tf_op jit(solution)/shard_map/dynamic_update_slice | solution.py:115
  287.1 11.2 %dynamic_update_slice.34 = bf16[1408,2048]{0,1:T(8,128)(2,1)} dynamic-update-slice(bf16[1408,2048]{0,1:T(8,128)(2,1)} %dynamic_update_slice.33, bf16[176,2048]{0,1:T(8,128)(2,1)S(1)} %copy.46, s32[]{:T(128)S(6)} %select_n.103, s32[]{:T(128)} %constant.138.clone.1) | dynamic-update-slice | bytes 1441796 | tf_op jit(solution)/shard_map/dynamic_update_slice | solution.py:110
  298.8 11.4 %dynamic_update_slice.35 = bf16[1408,2048]{0,1:T(8,128)(2,1)} dynamic-update-slice(bf16[1408,2048]{0,1:T(8,128)(2,1)} %dynamic_update_slice.34, bf16[176,2048]{0,1:T(8,128)(2,1)S(1)} %copy.47, s32[]{:T(128)S(6)} %select_n.105, s32[]{:T(128)} %constant.138.clone.1) | dynamic-update-slice | bytes 1441796 | tf_op jit(solution)/shard_map/dynamic_update_slice | solution.py:115
  310.7 11.4 %dynamic_update_slice.36 = bf16[1408,2048]{0,1:T(8,128)(2,1)} dynamic-update-slice(bf16[1408,2048]{0,1:T(8,128)(2,1)} %dynamic_update_slice.35, bf16[176,2048]{0,1:T(8,128)(2,1)S(1)} %copy.48, s32[]{:T(128)S(6)} %select_n.107, s32[]{:T(128)} %constant.138.clone.1) | dynamic-update-slice | bytes 1441796 | tf_op jit(solution)/shard_map/dynamic_update_slice | solution.py:110
  322.1 1.4 copy.49
  323.6 11.4 %dynamic_update_slice.37 = bf16[1408,2048]{0,1:T(8,128)(2,1)} dynamic-update-slice(bf16[1408,2048]{0,1:T(8,128)(2,1)} %dynamic_update_slice.36, bf16[176,2048]{0,1:T(8,128)(2,1)S(1)} %copy.49, s32[]{:T(128)S(6)} %select_n.109, s32[]{:T(128)} %constant.138.clone.1) | dynamic-update-slice | bytes 1441796 | tf_op jit(solution)/shard_map/dynamic_update_slice | solution.py:115
  335.0 1.4 copy.50
  336.4 11.4 %dynamic_update_slice.38 = bf16[1408,2048]{0,1:T(8,128)(2,1)} dynamic-update-slice(bf16[1408,2048]{0,1:T(8,128)(2,1)} %dynamic_update_slice.37, bf16[176,2048]{0,1:T(8,128)(2,1)S(1)} %copy.50, s32[]{:T(128)S(6)} %select_n.111, s32[]{:T(128)} %constant.138.clone.1) | dynamic-update-slice | bytes 1441796 | tf_op jit(solution)/shard_map/dynamic_update_slice | solution.py:110
  347.8 3.6 convert_reduce_fusion
  352.1 1.6 fusion.16
  353.8 4.0 fusion.18
  357.8 10.6 %reshape.116 = bf16[1408,512,4]{0,2,1:T(4,128)(2,1)} reshape(bf16[1408,2048]{0,1:T(8,128)(2,1)} %fusion.18) | data formatting | bytes 11534336 | tf_op jit(solution)/shard_map/reshape | solution.py:125
  368.4 5.4 %fusion.33 = bf16[176,512]{1,0:T(8,128)(2,1)} fusion(bf16[1408,512,4]{0,2,1:T(4,128)(2,1)} %reshape.116, bf16[22,4,8,1408]{3,2,1,0:T(8,128)(2,1)S(1)} %bitcast.67), kind=kOutput, calls=%fused_computation.32 | convolution fusion | flops 1015111680 | bytes 7929856 | tf_op jit(solution)/shard_map/ojf,fgj->og/dot_general | solution.py:127
  373.9 23.7 %all-gather = s32[16,1,512]{2,1,0:T(1,128)S(1)} all-gather(s32[1,1,512]{2,1,0:T(1,128)S(1)} %bitcast.65), channel_id=1, replica_groups=mesh['row'=16,'col'=8] {'row'}, dimensions={0}, use_global_device_ids=true | all-gather | bytes 34816 | tf_op jit(solution)/shard_map/all_gather | solution.py:133
  397.6 29.0 %all-gather.3.cloned.1.call-done = bf16[176,8192]{1,0:T(8,128)(2,1)} async-done(((bf16[176,512]{1,0:T(8,128)(2,1)}), bf16[176,8192]{1,0:T(8,128)(2,1)}) %all-gather.3.cloned.1.call-update) | async-done | bytes 2883600 | tf_op jit(solution)/shard_map/all_gather | solution.py:132
  426.5 5.8 %copy.53 = bf16[8192,176]{1,0:T(8,128)(2,1)} copy(bf16[8192,176]{0,1:T(8,128)(2,1)} %bitcast.60) | data formatting | bytes 5767168 | tf_op jit(solution)/shard_map/all_gather | solution.py:132
  432.3 35.2 %scatter_custom_fusion = bf16[176,512]{0,1:T(8,128)(2,1)S(1)} fusion(s32[8192]{0:T(1024)S(1)} %compare_select_fusion, bf16[8192,176]{1,0:T(8,128)(2,1)} %copy.53, bf16[]{:T(256)} %constant.140.clone.1), kind=kCustom, calls=%fused_computation.36 | custom fusion | bytes 180736 | tf_op jit(solution)/shard_map/scatter | solution.py:137
  (70 shorter events, 16.4 us)
Async XLA Ops:
  7.2 23.8 %slice-start = ((bf16[3,176,2048]{2,1,0:T(8,128)(2,1)}), bf16[2,176,2048]{2,1,0:T(8,128)(2,1)S(1)}, s32[]{:S(2)}) async-start(bf16[3,176,2048]{2,1,0:T(8,128)(2,1)} %param.9), calls=%async_computation.3 | async-start | bytes 2883584 | tf_op jit(solution)/shard_map/slice | solution.py:48
  7.2 9.2 %copy-start.9 = (s32[64]{0:T(128)S(1)}, s32[64]{0:T(128)}, u32[]{:S(2)}) copy-start(s32[64]{0:T(128)} %param.14) | copy-start | bytes 772
  7.2 202.4 %reduce-scatter.2.cloned.1.call-start = ((), (), s32[]{:S(2)}) async-start(), calls=%async_computation.1 | async-start | bytes 12976128 | tf_op jit(solution)/shard_map/reduce_scatter | solution.py:89
  9.7 20.2 %collective-permute-start.1 = (bf16[2,176,1024]{2,1,0:T(8,128)(2,1)}, bf16[2,176,1024]{2,1,0:T(8,128)(2,1)S(1)}, u32[]{:S(2)}, u32[]{:S(2)}) collective-permute-start(bf16[2,176,1024]{2,1,0:T(8,128)(2,1)} %get-tuple-element.107), channel_id=1, source_target_pairs={{8,0},{16,8},{24,16},{32,24},{40,32},{48,40},{56,48},{64,56},{72,6... | collective-permute-start | bytes 2162696 | tf_op jit(solution)/shard_map/ppermute | solution.py:20
  11.0 19.9 %collective-permute-start = (bf16[2,176,1024]{2,1,0:T(8,128)(2,1)S(1)}, bf16[2,176,1024]{2,1,0:T(8,128)(2,1)}, u32[]{:S(2)}, u32[]{:S(2)}) collective-permute-start(bf16[2,176,1024]{2,1,0:T(8,128)(2,1)S(1)} %get-tuple-element.106), channel_id=1, source_target_pairs={{0,8},{8,16},{16,24},{24,32},{32,40},{40,48},{48,56},{56,64},{64,7... | collective-permute-start | bytes 2162696 | tf_op jit(solution)/shard_map/ppermute | solution.py:18
  56.5 12.0 %copy-start.1 = (bf16[1,176,3072]{2,1,0:T(8,128)(2,1)S(1)}, bf16[1,176,3072]{2,1,0:T(8,128)(2,1)}, u32[]{:S(2)}) copy-start(bf16[1,176,3072]{2,1,0:T(8,128)(2,1)} %get-tuple-element.153) | copy-start | bytes 3244036 | tf_op jit(solution)/shard_map/while
  103.6 12.0 %copy-start.1 = (bf16[1,176,3072]{2,1,0:T(8,128)(2,1)S(1)}, bf16[1,176,3072]{2,1,0:T(8,128)(2,1)}, u32[]{:S(2)}) copy-start(bf16[1,176,3072]{2,1,0:T(8,128)(2,1)} %get-tuple-element.153) | copy-start | bytes 3244036 | tf_op jit(solution)/shard_map/while
  136.5 73.0 %copy-start.6 = (bf16[176,2048]{1,0:T(8,128)(2,1)S(1)}, bf16[176,2048]{1,0:T(8,128)(2,1)}, u32[]{:S(2)}) copy-start(bf16[176,2048]{1,0:T(8,128)(2,1)} %param.10) | copy-start | bytes 2162692
  136.5 290.0 %all-gather.3.cloned.1.call-start = ((), (), s32[]{:S(2)}) async-start(), calls=%async_computation.2 | async-start | bytes 3063808 | tf_op jit(solution)/shard_map/all_gather | solution.py:132
  211.1 51.0 %copy-start.2 = (bf16[176,2048]{1,0:T(8,128)(2,1)}, bf16[176,2048]{1,0:T(8,128)(2,1)S(1)}, u32[]{:S(2)}) copy-start(bf16[176,2048]{1,0:T(8,128)(2,1)S(1)} %add_convert_fusion) | copy-start | bytes 2162692
  211.1 11.9 %collective-permute-start.2 = (bf16[176,2048]{1,0:T(8,128)(2,1)S(1)}, bf16[176,2048]{1,0:T(8,128)(2,1)S(1)}, u32[]{:S(2)}, u32[]{:S(2)}) collective-permute-start(bf16[176,2048]{1,0:T(8,128)(2,1)S(1)} %add_convert_fusion), channel_id=1, source_target_pairs={{0,1},{1,2},{2,3},{3,4},{4,5},{5,6},{6,7},{7,0},{8,9},{9,10},{10,1... | collective-permute-start | bytes 2162696 | tf_op jit(solution)/shard_map/ppermute | solution.py:109
  211.1 11.9 %collective-permute-start.3 = (bf16[176,2048]{1,0:T(8,128)(2,1)S(1)}, bf16[176,2048]{1,0:T(8,128)(2,1)S(1)}, u32[]{:S(2)}, u32[]{:S(2)}) collective-permute-start(bf16[176,2048]{1,0:T(8,128)(2,1)S(1)} %add_convert_fusion), channel_id=1, source_target_pairs={{0,7},{1,0},{2,1},{3,2},{4,3},{5,4},{6,5},{7,6},{8,15},{9,8},{10,9... | collective-permute-start | bytes 2162696 | tf_op jit(solution)/shard_map/ppermute | solution.py:114
  223.0 3.0 copy-start.5
  223.0 11.9 %collective-permute-start.4 = (bf16[176,2048]{1,0:T(8,128)(2,1)S(1)}, bf16[176,2048]{1,0:T(8,128)(2,1)S(1)}, u32[]{:S(2)}, u32[]{:S(2)}) collective-permute-start(bf16[176,2048]{1,0:T(8,128)(2,1)S(1)} %collective-permute-done.2), channel_id=1, source_target_pairs={{0,1},{1,2},{2,3},{3,4},{4,5},{5,6},{6,7},{7,0},{8,9},{9,10},{10,1... | collective-permute-start | bytes 2162696 | tf_op jit(solution)/shard_map/ppermute | solution.py:109
  223.0 23.8 %copy-start.3 = (bf16[176,2048]{1,0:T(8,128)(2,1)}, bf16[176,2048]{1,0:T(8,128)(2,1)S(1)}, u32[]{:S(2)}) copy-start(bf16[176,2048]{1,0:T(8,128)(2,1)S(1)} %collective-permute-done.3) | copy-start | bytes 2162692
  223.0 11.9 %collective-permute-start.5 = (bf16[176,2048]{1,0:T(8,128)(2,1)S(1)}, bf16[176,2048]{1,0:T(8,128)(2,1)S(1)}, u32[]{:S(2)}, u32[]{:S(2)}) collective-permute-start(bf16[176,2048]{1,0:T(8,128)(2,1)S(1)} %collective-permute-done.3), channel_id=1, source_target_pairs={{0,7},{1,0},{2,1},{3,2},{4,3},{5,4},{6,5},{7,6},{8,15},{9,8},{10,9... | collective-permute-start | bytes 2162696 | tf_op jit(solution)/shard_map/ppermute | solution.py:114
  235.0 11.9 %copy-start.4 = (bf16[176,2048]{1,0:T(8,128)(2,1)}, bf16[176,2048]{1,0:T(8,128)(2,1)S(1)}, u32[]{:S(2)}) copy-start(bf16[176,2048]{1,0:T(8,128)(2,1)S(1)} %collective-permute-done.4) | copy-start | bytes 2162692
  235.0 11.9 %collective-permute-start.6 = (bf16[176,2048]{1,0:T(8,128)(2,1)S(1)}, bf16[176,2048]{1,0:T(8,128)(2,1)S(1)}, u32[]{:S(2)}, u32[]{:S(2)}) collective-permute-start(bf16[176,2048]{1,0:T(8,128)(2,1)S(1)} %collective-permute-done.4), channel_id=1, source_target_pairs={{0,1},{1,2},{2,3},{3,4},{4,5},{5,6},{6,7},{7,0},{8,9},{9,10},{10,1... | collective-permute-start | bytes 2162696 | tf_op jit(solution)/shard_map/ppermute | solution.py:109
  235.0 87.2 %collective-permute-start.7 = (bf16[176,2048]{1,0:T(8,128)(2,1)S(1)}, bf16[176,2048]{1,0:T(8,128)(2,1)}, u32[]{:S(2)}, u32[]{:S(2)}) collective-permute-start(bf16[176,2048]{1,0:T(8,128)(2,1)S(1)} %collective-permute-done.5), channel_id=1, source_target_pairs={{0,7},{1,0},{2,1},{3,2},{4,3},{5,4},{6,5},{7,6},{8,15},{9,8},{10,9... | collective-permute-start | bytes 2162696 | tf_op jit(solution)/shard_map/ppermute | solution.py:114
  246.9 88.1 %collective-permute-start.8 = (bf16[176,2048]{1,0:T(8,128)(2,1)S(1)}, bf16[176,2048]{1,0:T(8,128)(2,1)}, u32[]{:S(2)}, u32[]{:S(2)}) collective-permute-start(bf16[176,2048]{1,0:T(8,128)(2,1)S(1)} %collective-permute-done.6), channel_id=1, source_target_pairs={{0,1},{1,2},{2,3},{3,4},{4,5},{5,6},{6,7},{7,0},{8,9},{9,10},{10,1... | collective-permute-start | bytes 2162696 | tf_op jit(solution)/shard_map/ppermute | solution.py:109
  347.8 4.3 copy-start
  347.8 6.0 %copy-start.7 = (f32[1408]{0:T(1024)S(1)}, f32[1408]{0:T(1024)}, u32[]{:S(2)}) copy-start(f32[1408]{0:T(1024)} %param.13) | copy-start | bytes 16900
  357.8 10.6 %copy-start.10 = (bf16[176,5632]{1,0:T(8,128)(2,1)S(1)}, bf16[176,5632]{1,0:T(8,128)(2,1)}, u32[]{:S(2)}) copy-start(bf16[176,5632]{1,0:T(8,128)(2,1)} %param.12) | copy-start | bytes 5947396
  368.4 5.4 %copy-start.8 = (s32[512]{0:T(512)S(1)}, s32[512]{0:T(512)}, u32[]{:S(2)}) copy-start(s32[512]{0:T(512)} %param.15) | copy-start | bytes 6148
Sparse Core Ops, SparseCore 0:
  136.7 72.8 reduce-scatter.1
  374.0 52.5 all-gather.2
